TPU v7x, 256 devices: a whole 4x4x8 slice. The times are simulated.
256 devices in a mesh: replica: 8 (over x, core), outer: 4 (over y), link: 8 (over z).
Axes of the slice: x: 4, y: 4, z: 8, core: 2. Of those that a mesh axis runs over, the one named last changes fastest.
Arguments:
- link_in: bfloat16 [8, 16384, 256], P('replica', ('outer', 'link')), may hold values from -6 to 6
- path_in: bfloat16 [8, 4096, 256], P('replica', ('outer', 'link')), may hold values from -6 to 6
- hop_slots: int32 [8, 4096, 24], P('replica', ('outer', 'link')), may hold values from 0 to 2047
- hop_lens: int32 [8, 4096], P('replica', ('outer', 'link')), may hold values from 2 to 24
- failed: int32 [8, 16384], P('replica', ('outer', 'link')), may hold values 0 or 1
- serve_index: int32 [8, 32, 32, 64], P('replica', None, ('outer', 'link')), may hold values from 0 to 511
- link_grad: bfloat16 [8, 16384, 256], P('replica', ('outer', 'link')), may hold values from -6 to 6
- path_grad: bfloat16 [8, 4096, 256], P('replica', ('outer', 'link')), may hold values from -6 to 6
- gru_wx: bfloat16 [256, 768], replicated, may hold values from -0.375 to 0.375
- gru_wh: bfloat16 [256, 768], replicated, may hold values from -0.375 to 0.375
- gru_bias: float32 [768], replicated, may hold values from -3 to 3
- mlp_w1: bfloat16 [512, 256], replicated, may hold values from -0.25 to 0.25
- mlp_b1: float32 [256], replicated, may hold values from -3 to 3
- mlp_w2: bfloat16 [256, 256], replicated, may hold values from -0.375 to 0.375
- mlp_b2: float32 [256], replicated, may hold values from -3 to 3
Outputs:
- link_out: bfloat16 [8, 16384, 256], P('replica', ('outer', 'link'))
- path_out: bfloat16 [8, 4096, 256], P('replica', ('outer', 'link'))
- link_in_grad: float32 [8, 16384, 256], P('replica', ('outer', 'link'))
- path_in_grad: float32 [8, 4096, 256], P('replica', ('outer', 'link'))
- grad_wx: float32 [256, 768], replicated
- grad_wh: float32 [256, 768], replicated
- grad_bias: float32 [768], replicated
- grad_w1: float32 [512, 256], replicated
- grad_b1: float32 [256], replicated
- grad_w2: float32 [256, 256], replicated
- grad_b2: float32 [256], replicated
Inputs may be any that keep to these rules, and one draw needn't show every extreme that they name: `serve_index`: entry [s, d, o, c] names, among the 512 links of owner device o, the link in request slot c of device d; a link may fill several slots. `hop_slots`: slot o * 64 + c is request slot c of the flow's own device towards owner o; entries at hops past the flow's length are ignored. 1 marks a failed link.
All inputs are finite; a program needn't handle non-finite values. No bound on the sum of `failed` on one device may be relied on, other than what follows from the above.
Results may differ from a plain program's by a relative error of at most 0.0067.
Values may be sent and summed in bfloat16 or wider, within the bound.
No kernel may reach another device: no remote copies, remote signals or barrier semaphores. Data moves between devices by JAX's collectives and lax.ppermute only.
A program may use at most 128 MiB of HBM per device.

v0:
```python
import jax
import jax.numpy as jnp
from jax import lax
from jax.sharding import PartitionSpec as P


def gate_terms(state_now, hop_input, input_weight, hidden_weight, gate_bias):
    from_input = jnp.dot(hop_input, input_weight, preferred_element_type=jnp.float32) + gate_bias
    from_state = jnp.dot(
        state_now.astype(jnp.bfloat16), hidden_weight, preferred_element_type=jnp.float32
    )
    return (from_input, from_state)


def gru_cell(state_now, from_input, from_state):
    feat_width = state_now.shape[1]
    update = jax.nn.sigmoid(from_input[:, :feat_width] + from_state[:, :feat_width])
    reset = jax.nn.sigmoid(
        from_input[:, feat_width : 2 * feat_width] + from_state[:, feat_width : 2 * feat_width]
    )
    candidate = jnp.tanh(from_input[:, 2 * feat_width :] + reset * from_state[:, 2 * feat_width :])
    return (candidate + update * (state_now - candidate), update, reset, candidate)


def gru_forward(path_start, hop_inputs, live_mask, input_weight, hidden_weight, gate_bias):

    def advance(state_now, scan_item):
        hop_input, live_now = scan_item
        from_input, from_state = gate_terms(
            state_now, hop_input, input_weight, hidden_weight, gate_bias
        )
        stepped = gru_cell(state_now, from_input, from_state)[0]
        state_next = jnp.where(live_now[:, None] > 0, stepped, state_now)
        return (state_next, (state_next,))

    return lax.scan(advance, path_start.astype(jnp.float32), (hop_inputs, live_mask))[1]


def back_step(
    carried, hop_input, state_now, live_now, hop_grad, from_input, from_state, input_tr, hidden_tr
):
    grad_state, grad_wx, grad_wh, grad_bias = carried
    feat_width = state_now.shape[1]
    live_col = live_now[:, None]
    grad_state = grad_state + live_col * hop_grad
    update, reset, candidate = gru_cell(state_now, from_input, from_state)[1:]
    pre_update = grad_state * (state_now - candidate) * update * (1.0 - update)
    pre_cand = grad_state * (1.0 - update) * (1.0 - candidate * candidate)
    pre_reset = pre_cand * from_state[:, 2 * feat_width :] * reset * (1.0 - reset)
    grad_in = jnp.concatenate([pre_update, pre_reset, pre_cand], axis=1) * live_col
    grad_hid = jnp.concatenate([pre_update, pre_reset, pre_cand * reset], axis=1) * live_col
    in_bf = grad_in.astype(jnp.bfloat16)
    hid_bf = grad_hid.astype(jnp.bfloat16)
    grad_prev = jnp.where(
        live_col > 0,
        grad_state * update + jnp.dot(hid_bf, hidden_tr, preferred_element_type=jnp.float32),
        grad_state,
    )
    grad_input = jnp.dot(in_bf, input_tr, preferred_element_type=jnp.float32)
    grad_wx = grad_wx + jnp.dot(hop_input.T, in_bf, preferred_element_type=jnp.float32)
    grad_wh = grad_wh + jnp.dot(
        state_now.astype(jnp.bfloat16).T, hid_bf, preferred_element_type=jnp.float32
    )
    grad_bias = grad_bias + jnp.sum(grad_in, axis=0)
    return ((grad_prev, grad_wx, grad_wh, grad_bias), grad_input)


def gru_backward(
    path_start,
    states,
    hop_inputs,
    live_mask,
    hop_grads,
    path_grad,
    input_weight,
    hidden_weight,
    gate_bias,
):
    feat_width = path_start.shape[1]
    prior_states = jnp.concatenate([path_start.astype(jnp.float32)[None], states[:-1]], axis=0)
    input_tr = input_weight.T
    hidden_tr = hidden_weight.T
    initial = (
        path_grad.astype(jnp.float32),
        jnp.zeros((feat_width, 3 * feat_width), jnp.float32),
        jnp.zeros((feat_width, 3 * feat_width), jnp.float32),
        jnp.zeros((3 * feat_width,), jnp.float32),
    )

    def retreat(carried, scan_item):
        hop_input, state_now, live_now, hop_grad = scan_item
        from_input, from_state = gate_terms(
            state_now, hop_input, input_weight, hidden_weight, gate_bias
        )
        return back_step(
            carried,
            hop_input,
            state_now,
            live_now,
            hop_grad,
            from_input,
            from_state,
            input_tr,
            hidden_tr,
        )

    scan_items = (hop_inputs, prior_states, live_mask, hop_grads)
    return lax.scan(retreat, initial, scan_items, reverse=True)


def link_forward(link_rows, agg_bf, keep_col, mlp_w1, mlp_b1, mlp_w2, mlp_b2):
    feat_width = link_rows.shape[1]
    pre_act = (
        jnp.dot(link_rows, mlp_w1[:feat_width], preferred_element_type=jnp.float32)
        + jnp.dot(agg_bf, mlp_w1[feat_width:], preferred_element_type=jnp.float32)
        + mlp_b1
    )
    activ = jax.nn.silu(pre_act).astype(jnp.bfloat16)
    value = (
        link_rows.astype(jnp.float32)
        + jnp.dot(activ, mlp_w2, preferred_element_type=jnp.float32)
        + mlp_b2
    )
    return ((keep_col * value).astype(jnp.bfloat16), pre_act, activ)


def link_backward(link_grad_rows, link_rows, agg_bf, keep_col, pre_act, activ, mlp_w1, mlp_w2):
    feat_width = link_rows.shape[1]
    grad_val = keep_col * link_grad_rows.astype(jnp.float32)
    val_bf = grad_val.astype(jnp.bfloat16)
    grad_w2 = jnp.dot(activ.T, val_bf, preferred_element_type=jnp.float32)
    grad_b2 = jnp.sum(grad_val, axis=0)
    grad_act = jnp.dot(val_bf, mlp_w2.T, preferred_element_type=jnp.float32)
    sigma = jax.nn.sigmoid(pre_act)
    grad_pre = grad_act * sigma * (1.0 + pre_act * (1.0 - sigma))
    pre_bf = grad_pre.astype(jnp.bfloat16)
    grad_w1 = jnp.concatenate(
        [
            jnp.dot(link_rows.T, pre_bf, preferred_element_type=jnp.float32),
            jnp.dot(agg_bf.T, pre_bf, preferred_element_type=jnp.float32),
        ],
        axis=0,
    )
    grad_b1 = jnp.sum(grad_pre, axis=0)
    link_direct = grad_val + jnp.dot(
        pre_bf, mlp_w1[:feat_width].T, preferred_element_type=jnp.float32
    )
    agg_grad = jnp.dot(pre_bf, mlp_w1[feat_width:].T, preferred_element_type=jnp.float32).astype(
        jnp.bfloat16
    )
    return (link_direct, agg_grad, (grad_w1, grad_b1, grad_w2, grad_b2))


def swap_slots(blocks):
    return lax.all_to_all(blocks, ("outer", "link"), split_axis=0, concat_axis=0, tiled=True)


def body(
    link_in,
    path_in,
    hop_slots,
    hop_lens,
    failed,
    serve_index,
    link_grad,
    path_grad,
    gru_wx,
    gru_wh,
    gru_bias,
    mlp_w1,
    mlp_b1,
    mlp_w2,
    mlp_b2,
):
    link_rows = link_in[0]
    feat_width = link_rows.shape[1]
    link_count = link_rows.shape[0]
    serve_rows = serve_index[0, :, 0, :]
    group_size, slot_cap = serve_rows.shape
    serve_flat = serve_rows.reshape(-1)
    slot_ids = hop_slots[0].T
    hop_count, flow_count = slot_ids.shape
    flat_slots = slot_ids.reshape(-1)
    live_mask = (jnp.arange(hop_count, dtype=jnp.int32)[:, None] < hop_lens[0][None, :]).astype(
        jnp.float32
    )
    fetched = swap_slots(jnp.take(link_rows, serve_rows, axis=0))
    hop_inputs = jnp.take(fetched.reshape(group_size * slot_cap, feat_width), slot_ids, axis=0)
    states = gru_forward(path_in[0], hop_inputs, live_mask, gru_wx, gru_wh, gru_bias)[0]
    partial_value = jax.ops.segment_sum(
        (states * live_mask[:, :, None]).reshape(hop_count * flow_count, feat_width),
        flat_slots,
        num_segments=group_size * slot_cap,
    ).astype(jnp.bfloat16)
    arrived = swap_slots(partial_value.reshape(group_size, slot_cap, feat_width))
    aggregate = jax.ops.segment_sum(
        arrived.reshape(group_size * slot_cap, feat_width).astype(jnp.float32),
        serve_flat,
        num_segments=link_count,
    )
    agg_bf = aggregate.astype(jnp.bfloat16)
    keep_col = (1 - failed[0]).astype(jnp.float32)[:, None]
    link_out, pre_act, activ = link_forward(
        link_rows, agg_bf, keep_col, mlp_w1, mlp_b1, mlp_w2, mlp_b2
    )
    path_out = states[-1].astype(jnp.bfloat16)
    link_direct, agg_grad, mlp_terms = link_backward(
        link_grad[0], link_rows, agg_bf, keep_col, pre_act, activ, mlp_w1, mlp_w2
    )
    returned = swap_slots(jnp.take(agg_grad, serve_rows, axis=0))
    hop_grads = (
        jnp.take(returned.reshape(group_size * slot_cap, feat_width), slot_ids, axis=0).astype(
            jnp.float32
        )
        * live_mask[:, :, None]
    )
    finished, grad_inputs = gru_backward(
        path_in[0], states, hop_inputs, live_mask, hop_grads, path_grad[0], gru_wx, gru_wh, gru_bias
    )
    dpart = jax.ops.segment_sum(
        grad_inputs.reshape(hop_count * flow_count, feat_width),
        flat_slots,
        num_segments=group_size * slot_cap,
    ).astype(jnp.bfloat16)
    owned = swap_slots(dpart.reshape(group_size, slot_cap, feat_width))
    link_back = link_direct + jax.ops.segment_sum(
        owned.reshape(group_size * slot_cap, feat_width).astype(jnp.float32),
        serve_flat,
        num_segments=link_count,
    )
    summed = lax.psum(
        (
            finished[1],
            finished[2],
            finished[3],
            mlp_terms[0],
            mlp_terms[1],
            mlp_terms[2],
            mlp_terms[3],
        ),
        ("replica", "outer", "link"),
    )
    device_count = lax.axis_size("replica") * lax.axis_size("outer") * lax.axis_size("link")
    grad_scale = float(device_count * link_count) ** (-0.5)
    return (
        link_out[None],
        path_out[None],
        link_back[None],
        finished[0][None],
        summed[0] * grad_scale,
        summed[1] * grad_scale,
        summed[2] * grad_scale,
        summed[3] * grad_scale,
        summed[4] * grad_scale,
        summed[5] * grad_scale,
        summed[6] * grad_scale,
    )


def solution(mesh):
    return jax.shard_map(
        body,
        mesh=mesh,
        in_specs=(
            P("replica", ("outer", "link"), None),
            P("replica", ("outer", "link"), None),
            P("replica", ("outer", "link"), None),
            P("replica", ("outer", "link")),
            P("replica", ("outer", "link")),
            P("replica", None, ("outer", "link"), None),
            P("replica", ("outer", "link"), None),
            P("replica", ("outer", "link"), None),
            P(),
            P(),
            P(),
            P(),
            P(),
            P(),
            P(),
        ),
        out_specs=(
            P("replica", ("outer", "link"), None),
            P("replica", ("outer", "link"), None),
            P("replica", ("outer", "link"), None),
            P("replica", ("outer", "link"), None),
            P(),
            P(),
            P(),
            P(),
            P(),
            P(),
            P(),
        ),
        check_vma=False,
    )
```

profile of v0, /device:TPU:2, one launch (start us, length us, event | category | flops | bytes accessed | tf_op | source)
XLA Modules:
  0.0 706.7 jit_solution(12861078215785412026)
XLA Ops:
  8.8 7.6 %gather_fusion = bf16[2048,256]{1,0:T(8,128)(2,1)S(1)} fusion(bf16[512,256]{1,0:T(8,128)(2,1)} %bitcast.135, s32[2048]{0:T(1024)S(1)} %broadcast_clamp_fusion), kind=kCustom, calls=%fused_computation.clone | custom fusion | bytes 2105344 | tf_op jit(solution)/shard_map/jit(_take)/gather | solution.py:187
  16.4 1.2 broadcast_select_fusion.2
  17.7 11.5 %all-to-all-start = ((bf16[32,64,256]{2,1,0:T(8,128)(2,1)}), bf16[32,64,256]{2,1,0:T(8,128)(2,1)S(1)}, u32[]{:S(2)}, u32[]{:S(2)}) async-start(bf16[32,64,256]{2,1,0:T(8,128)(2,1)} %broadcast_select_fusion.2), calls=%async_computation | async-start | bytes 2097152 | tf_op jit(solution)/shard_map/all_to_all | solution.py:155
  29.9 27.9 %all-to-all-done = bf16[32,64,256]{2,1,0:T(8,128)(2,1)S(1)} async-done(((bf16[32,64,256]{2,1,0:T(8,128)(2,1)}), bf16[32,64,256]{2,1,0:T(8,128)(2,1)S(1)}, u32[]{:S(2)}, u32[]{:S(2)}) %all-to-all-start) | async-done | bytes 1048608 | tf_op jit(solution)/shard_map/all_to_all | solution.py:155
  57.8 13.0 %gather_fusion.1 = bf16[3072,256]{1,0:T(8,128)(2,1)} fusion(bf16[2048,256]{1,0:T(8,128)(2,1)S(1)} %bitcast.137, s32[3072]{0:T(1024)S(1)} %bitcast_clamp_fusion), kind=kCustom, calls=%fused_computation.1.clone | custom fusion | bytes 3158016 | tf_op jit(solution)/shard_map/jit(_take)/gather | solution.py:188
  70.7 1.7 broadcast_select_fusion
  72.5 2.0 broadcast.84.clone
  74.6 29.4 %while.35 = (s32[]{:T(128)}, f32[128,256]{1,0:T(8,128)S(1)}, f32[24,128,256]{2,1,0:T(8,128)}, f32[24,128]{1,0:T(8,128)S(1)}, bf16[24,128,256]{2,1,0:T(8,128)(2,1...) while((s32[]{:T(128)}, f32[128,256]{1,0:T(8,128)S(1)}, ...), condition=%wide.region_1.4_spmd, body=%wide.region_0.3_spmd.sunk | while | flops 101253248 | bytes 2954097 | solution.py:36
  104.0 4.6 broadcast_multiply_fusion
  108.5 17.9 %scatter_custom_fusion = f32[2048,256]{1,0:T(8,128)S(1)} fusion(s32[3072]{0:T(1024)S(1)} %bitcast.155, f32[3072,256]{1,0:T(8,128)} %bitcast.148, f32[]{:T(128)} %constant.108.clone.1), kind=kCustom, calls=%fused_computation.102 | custom fusion | flops 786432 | bytes 2097664 | tf_op jit(solution)/shard_map/scatter-add | solution.py:190
  127.6 5.2 all-to-all-start.1
  135.5 25.6 %all-to-all-done.1 = bf16[32,64,256]{2,1,0:T(8,128)(2,1)S(1)} async-done(((bf16[32,64,256]{2,1,0:T(8,128)(2,1)}), bf16[32,64,256]{2,1,0:T(8,128)(2,1)S(1)}, u32[]{:S(2)}, u32[]{:S(2)}) %all-to-all-start.1) | async-done | bytes 1048608 | tf_op jit(solution)/shard_map/all_to_all | solution.py:155
  161.1 11.9 %scatter_custom_fusion.1 = f32[512,256]{1,0:T(8,128)S(1)} fusion(s32[2048]{0:T(1024)} %reshape.174, bf16[2048,256]{1,0:T(8,128)(2,1)S(1)} %bitcast.146, f32[]{:T(128)} %constant.108.clone.1), kind=kCustom, calls=%fused_computation.84 | custom fusion | flops 1048576 | bytes 1573376 | tf_op jit(solution)/shard_map/scatter-add | solution.py:196
  173.9 2.1 fusion.85
  177.0 7.5 %gather_fusion.2 = bf16[2048,256]{1,0:T(8,128)(2,1)S(1)} fusion(bf16[512,256]{1,0:T(8,128)(2,1)S(1)} %convolution_convert_fusion, s32[2048]{0:T(1024)S(1)} %broadcast_clamp_fusion), kind=kCustom, calls=%fused_computation.2.clone | custom fusion | bytes 2105344 | tf_op jit(solution)/shard_map/jit(_take)/gather | solution.py:210
  184.5 1.2 broadcast_select_fusion.1
  185.7 4.9 all-to-all-start.2
  192.7 1.5 bitcast_convert_fusion.3
  194.2 2.1 slice.91
  196.4 1.8 pad_maximum_fusion.1
  200.7 18.2 %all-to-all-done.2 = bf16[32,64,256]{2,1,0:T(8,128)(2,1)S(1)} async-done(((bf16[32,64,256]{2,1,0:T(8,128)(2,1)}), bf16[32,64,256]{2,1,0:T(8,128)(2,1)S(1)}, u32[]{:S(2)}, u32[]{:S(2)}) %all-to-all-start.2) | async-done | bytes 1048608 | tf_op jit(solution)/shard_map/all_to_all | solution.py:155
  218.9 12.9 %gather_fusion.3 = bf16[3072,256]{1,0:T(8,128)(2,1)} fusion(bf16[2048,256]{1,0:T(8,128)(2,1)S(1)} %bitcast.136, s32[3072]{0:T(1024)S(1)} %copy-done.32), kind=kCustom, calls=%fused_computation.3.clone | custom fusion | bytes 3158016 | tf_op jit(solution)/shard_map/jit(_take)/gather | solution.py:212
  231.9 4.1 convert_multiply_fusion
  236.0 2.1 broadcast.84
  238.1 176.1 %while.36 = (s32[]{:T(128)}, f32[128,256]{1,0:T(8,128)S(1)}, f32[256,768]{1,0:T(8,128)S(1)}, f32[256,768]{1,0:T(8,128)S(1)}, f32[768]{0:T(1024)S(1)}, /*index=5*...) while((s32[]{:T(128)}, f32[128,256]{1,0:T(8,128)S(1)}, ...), condition=%wide.region_6.9_spmd.clone, body=%wide.region_4.8_spmd.clone.sunk | while | flops 306152320 | bytes 12996093 | solution.py:108
  242.0 1.3 convolution_add_fusion.15
  243.3 1.2 convolution_add_fusion.14
  249.3 1.3 convolution_add_fusion.15
  256.7 1.3 convolution_add_fusion.15
  264.0 1.3 convolution_add_fusion.15
  265.3 1.2 convolution_add_fusion.14
  271.3 1.3 convolution_add_fusion.15
  272.6 1.2 convolution_add_fusion.14
  278.6 1.3 convolution_add_fusion.15
  279.9 1.2 convolution_add_fusion.14
  286.0 1.3 convolution_add_fusion.15
  293.3 1.3 convolution_add_fusion.15
  294.6 1.2 convolution_add_fusion.14
  300.7 1.3 convolution_add_fusion.15
  308.0 1.3 convolution_add_fusion.15
  315.3 1.3 convolution_add_fusion.15
  322.7 1.3 convolution_add_fusion.15
  330.0 1.3 convolution_add_fusion.15
  337.4 1.3 convolution_add_fusion.15
  344.7 1.3 convolution_add_fusion.15
  352.0 1.3 convolution_add_fusion.15
  359.4 1.3 convolution_add_fusion.15
  366.7 1.3 convolution_add_fusion.15
  368.0 1.2 convolution_add_fusion.14
  374.0 1.3 convolution_add_fusion.15
  381.4 1.3 convolution_add_fusion.15
  382.7 1.2 convolution_add_fusion.14
  388.7 1.3 convolution_add_fusion.15
  396.0 1.3 convolution_add_fusion.15
  403.4 1.3 convolution_add_fusion.15
  410.7 1.3 convolution_add_fusion.15
  415.5 1.5 slice.215
  417.0 17.9 %scatter_custom_fusion.2 = f32[2048,256]{1,0:T(8,128)S(1)} fusion(s32[3072]{0:T(1024)} %bitcast.154, f32[3072,256]{1,0:T(8,128)} %bitcast.147, f32[]{:T(128)} %constant.108.clone.1), kind=kCustom, calls=%fused_computation.100 | custom fusion | flops 786432 | bytes 2097664 | tf_op jit(solution)/shard_map/scatter-add | solution.py:220
  436.0 5.1 all-to-all-start.3
  442.4 76.8 %all-reduce = (f32[768]{0:T(1024)S(1)}, f32[256]{0:T(256)S(1)}, f32[256]{0:T(256)S(1)}) all-reduce(f32[768]{0:T(1024)S(1)} %get-tuple-element.357, f32[256]{0:T(256)S(1)} %copy-done.39, f32[256]{0:T(256)S(1)} %fusion.64), channel_id=1, replica_groups=mesh['replica'=8,'outer'=4,'link'=8] {'replica','outer','link'}, use_global_device_ids=true, to_apply=%region_11.14 | all-reduce | flops 1280 | bytes 10240 | tf_op jit(solution)/shard_map/psum | solution.py:231
  520.9 160.5 %all-reduce.4.cloned.1.call-done = (f32[256,768]{1,0:T(8,128)}, f32[256,768]{1,0:T(8,128)}, f32[512,256]{1,0:T(8,128)}, f32[256,256]{1,0:T(8,128)}) async-done(((f32[256,768]{1,0:T(8,128)}, f32[256,768]{1,0:T(8,128)}, f32[512,256]{1,0:T(8,128)}, f32[256,256]{1,0:T(8,128)}), (f32[256,768]{1,0:T(8,128)}, f32[256,768]{1,0:T(8,128)}, f32[512,256]{1,0:T(8,128)}, ...) | async-done | bytes 2359312 | tf_op jit(solution)/shard_map/psum | solution.py:231
  681.5 1.8 broadcast_multiply_fusion.4
  683.3 1.9 broadcast_multiply_fusion.3
  687.1 12.0 %scatter_custom_fusion.3 = f32[512,256]{1,0:T(8,128)S(1)} fusion(f32[512,256]{1,0:T(8,128)S(1)} %convolution_add_fusion.5, s32[2048]{0:T(1024)} %reshape.174, bf16[2048,256]{1,0:T(8,128)(2,1)S(1)} %bitcast.145), kind=kCustom, calls=%fused_computation.82 | custom fusion | flops 1048576 | bytes 1572864 | tf_op jit(solution)/shard_map/scatter-add | solution.py:226
  (519 shorter events, 184.1 us)
Async XLA Ops:
  7.2 166.7 %copy-start = (bf16[256,256]{1,0:T(8,128)(2,1)S(1)}, bf16[256,256]{1,0:T(8,128)(2,1)}, u32[]{:S(2)}) copy-start(bf16[256,256]{1,0:T(8,128)(2,1)} %param.36) | copy-start | bytes 393220
  16.4 12.8 %copy-start.34 = (s32[1,128,24]{1,2,0:T(8,128)S(1)}, s32[1,128,24]{1,2,0:T(8,128)}, u32[]{:S(2)}) copy-start(s32[1,128,24]{1,2,0:T(8,128)} %param.25) | copy-start | bytes 36868
  16.4 12.8 %copy-start.40 = (s32[1,128]{1,0:T(1,128)S(1)}, s32[1,128]{1,0:T(1,128)}, u32[]{:S(2)}) copy-start(s32[1,128]{1,0:T(1,128)} %param.26) | copy-start | bytes 1540
  16.4 12.8 %copy-start.33 = (bf16[1,128,256]{2,1,0:T(8,128)(2,1)S(1)}, bf16[1,128,256]{2,1,0:T(8,128)(2,1)}, u32[]{:S(2)}) copy-start(bf16[1,128,256]{2,1,0:T(8,128)(2,1)} %param.24) | copy-start | bytes 196612
  17.7 40.1 %all-to-all-start = ((bf16[32,64,256]{2,1,0:T(8,128)(2,1)}), bf16[32,64,256]{2,1,0:T(8,128)(2,1)S(1)}, u32[]{:S(2)}, u32[]{:S(2)}) async-start(bf16[32,64,256]{2,1,0:T(8,128)(2,1)} %broadcast_select_fusion.2), calls=%async_computation | async-start | bytes 2097152 | tf_op jit(solution)/shard_map/all_to_all | solution.py:155
  29.2 41.6 %copy-start.31 = (s32[3072]{0:T(1024)}, s32[3072]{0:T(1024)S(1)}, u32[]{:S(2)}) copy-start(s32[3072]{0:T(1024)S(1)} %bitcast_clamp_fusion) | copy-start | bytes 36868
  29.2 41.5 %copy-start.35 = (pred[24,128]{1,0:T(8,128)(4,1)}, pred[24,128]{1,0:T(8,128)(4,1)S(1)}, u32[]{:S(2)}) copy-start(pred[24,128]{1,0:T(8,128)(4,1)S(1)} %get-tuple-element.474) | copy-start | bytes 9220
  72.5 2.1 copy-start.2
  72.5 2.1 copy-start.3
  72.5 2.1 copy-start.25
  104.0 4.6 copy-start.12
  104.0 4.6 copy-start.29
  126.5 8.8 %copy-start.1 = (bf16[1,512,256]{2,1,0:T(8,128)(2,1)S(1)}, bf16[1,512,256]{2,1,0:T(8,128)(2,1)}, u32[]{:S(2)}) copy-start(bf16[1,512,256]{2,1,0:T(8,128)(2,1)} %param.23) | copy-start | bytes 786436
  126.5 8.8 %copy-start.13 = (bf16[512,256]{1,0:T(8,128)(2,1)S(1)}, bf16[512,256]{1,0:T(8,128)(2,1)}, u32[]{:S(2)}) copy-start(bf16[512,256]{1,0:T(8,128)(2,1)} %param.34) | copy-start | bytes 786436
  127.6 5.8 copy-start.28
  127.6 7.1 %copy-start.38 = (s32[1,512]{1,0:T(1,128)S(1)}, s32[1,512]{1,0:T(1,128)}, u32[]{:S(2)}) copy-start(s32[1,512]{1,0:T(1,128)} %param.27) | copy-start | bytes 6148
  127.6 45.4 %copy-start.14 = (bf16[512,256]{1,0:T(8,128)(2,1)S(1)}, bf16[512,256]{1,0:T(8,128)(2,1)}, u32[]{:S(2)}) copy-start(bf16[512,256]{1,0:T(8,128)(2,1)} %param.34) | copy-start | bytes 786436
  127.6 33.5 %all-to-all-start.1 = ((bf16[32,64,256]{2,1,0:T(8,128)(2,1)}), bf16[32,64,256]{2,1,0:T(8,128)(2,1)S(1)}, u32[]{:S(2)}, u32[]{:S(2)}) async-start(bf16[32,64,256]{2,1,0:T(8,128)(2,1)} %bitcast.142), calls=%async_computation.1 | async-start | bytes 2097152 | tf_op jit(solution)/shard_map/all_to_all | solution.py:155
  173.9 2.1 copy-start.20
  185.7 33.2 %all-to-all-start.2 = ((bf16[32,64,256]{2,1,0:T(8,128)(2,1)}), bf16[32,64,256]{2,1,0:T(8,128)(2,1)S(1)}, u32[]{:S(2)}, u32[]{:S(2)}) async-start(bf16[32,64,256]{2,1,0:T(8,128)(2,1)} %broadcast_select_fusion.1), calls=%async_computation.2 | async-start | bytes 2097152 | tf_op jit(solution)/shard_map/all_to_all | solution.py:155
  190.6 490.8 %all-reduce.4.cloned.1.call-start = ((), (), s32[]{:S(2)}) async-start(), calls=%async_computation.4 | async-start | bytes 4718592 | tf_op jit(solution)/shard_map/psum | solution.py:231
  194.2 2.1 copy-start.23
  196.3 1.8 copy-start.10
  198.2 1.4 copy-start.16
  198.2 1.4 copy-start.21
  198.2 1.4 copy-start.37
  198.8 20.2 %copy-start.32 = (s32[3072]{0:T(1024)S(1)}, s32[3072]{0:T(1024)}, u32[]{:S(2)}) copy-start(s32[3072]{0:T(1024)} %copy-done.31) | copy-start | bytes 36868
  218.9 12.9 %copy-start.30 = (f32[24,128]{1,0:T(8,128)S(1)}, f32[24,128]{1,0:T(8,128)}, u32[]{:S(2)}) copy-start(f32[24,128]{1,0:T(8,128)} %copy-done.29) | copy-start | bytes 36868
  218.9 13.0 %copy-start.36 = (pred[24,128]{1,0:T(8,128)(4,1)S(1)}, pred[24,128]{1,0:T(8,128)(4,1)}, u32[]{:S(2)}) copy-start(pred[24,128]{1,0:T(8,128)(4,1)} %copy-done.35) | copy-start | bytes 9220
  236.0 2.1 copy-start.5
  236.0 2.1 copy-start.7
  236.0 2.1 copy-start.26
  239.2 2.4 copy-start.27
  246.6 2.4 copy-start.27
  253.9 2.4 copy-start.27
  261.2 2.4 copy-start.27
  268.6 2.4 copy-start.27
  275.9 2.4 copy-start.27
  283.2 2.4 copy-start.27
  290.6 2.4 copy-start.27
  297.9 2.4 copy-start.27
  305.2 2.4 copy-start.27
  312.6 2.4 copy-start.27
  319.9 2.4 copy-start.27
  327.2 2.4 copy-start.27
  334.6 2.4 copy-start.27
  341.9 2.4 copy-start.27
  349.3 2.4 copy-start.27
  356.6 2.4 copy-start.27
  363.9 2.4 copy-start.27
  371.3 2.4 copy-start.27
  378.6 2.4 copy-start.27
  385.9 2.4 copy-start.27
  393.3 2.4 copy-start.27
  400.6 2.4 copy-start.27
  407.9 2.4 copy-start.27
  414.1 20.8 %copy-start.8 = (f32[128,256]{1,0:T(8,128)}, f32[128,256]{1,0:T(8,128)S(1)}, u32[]{:S(2)}) copy-start(f32[128,256]{1,0:T(8,128)S(1)} %get-tuple-element.354) | copy-start | bytes 393220
  434.9 6.2 copy-start.41
  436.0 5.1 copy-start.22
  436.0 6.1 copy-start.11
  436.0 6.1 copy-start.15
  436.0 251.0 %all-to-all-start.3 = ((bf16[32,64,256]{2,1,0:T(8,128)(2,1)}), bf16[32,64,256]{2,1,0:T(8,128)(2,1)S(1)}, u32[]{:S(2)}, u32[]{:S(2)}) async-start(bf16[32,64,256]{2,1,0:T(8,128)(2,1)} %bitcast.141), calls=%async_computation.3 | async-start | bytes 2097152 | tf_op jit(solution)/shard_map/all_to_all | solution.py:155
  681.5 3.7 copy-start.19
  681.5 4.6 copy-start.18
  (6 other events, 6.0 us)
Sparse Core Ops, SparseCore 0:
  415.4 265.9 all-reduce.3
where the time goes:
time: 711 us; the launch traced here: 707 us
  waiting for transfers between devices  232 us (33%)
  matrix products  158 us (22%)
  other arithmetic  141 us (20%)
  blocking collectives  76.8 us (11%)
  local copies, waits for them, and re-layouts  54.8 us (8%)
  starting transfers between devices  26.9 us (4%)
  between operations  14.5 us (2%)
    psum x1, waiting for transfers between devices, body(): lax.psum((finished[1], finished[2], finished[3], mlp_terms[0], mlp_terms[...  161 us
    psum x1, blocking collectives, body(): lax.psum((finished[1], finished[2], finished[3], mlp_terms[0], mlp_terms[...  76.8 us
    all_to_all x4, waiting for transfers between devices, swap_slots(): lax.all_to_all(blocks, ('outer', 'link'), split_axis=0, concat_axis=0, ti...  71.6 us
    dot_general x48, matrix products, gate_terms(): jnp.dot(hop_input, input_weight, preferred_element_type=jnp.float32)  31.8 us
    dot_general x48, matrix products, gate_terms(): jnp.dot(state_now.astype(jnp.bfloat16), hidden_weight, preferred_element_...  31.7 us
    dot_general x24, matrix products, back_step(): jnp.dot(state_now.astype(jnp.bfloat16).T, hid_bf, preferred_element_type=...  31 us
    dot_general x24, matrix products, back_step(): jnp.dot(hop_input.T, in_bf, preferred_element_type=jnp.float32)  29.4 us
    all_to_all x4, starting transfers between devices, swap_slots(): lax.all_to_all(blocks, ('outer', 'link'), split_axis=0, concat_axis=0, ti...  26.7 us
  transfers between devices with their start and end apart: 5, of which 4 were waited for; matrix products, arithmetic and copies ran while one was open for 6% of the time, Pallas kernels for 0%

commit v1 on v0

--- a/solution.py
+++ b/solution.py
@@ -172,6 +172,12 @@
     mlp_w2,
     mlp_b2,
 ):
+
+    def detail_sectors_over_axis(panel, axis_name, axis_tag):
+        for at in (axis_name, axis_tag):
+            panel = lax.psum(panel, at)
+        return panel
+
     link_rows = link_in[0]
     feat_width = link_rows.shape[1]
     link_count = link_rows.shape[0]
@@ -228,7 +234,7 @@
         serve_flat,
         num_segments=link_count,
     )
-    summed = lax.psum(
+    summed = detail_sectors_over_axis(
         (
             finished[1],
             finished[2],
@@ -238,7 +244,8 @@
             mlp_terms[2],
             mlp_terms[3],
         ),
-        ("replica", "outer", "link"),
+        ("outer", "link"),
+        "replica",
     )
     device_count = lax.axis_size("replica") * lax.axis_size("outer") * lax.axis_size("link")
     grad_scale = float(device_count * link_count) ** (-0.5)

time: 711 us -> 699 us (0.983)
  waiting for transfers between devices: 232 us -> 211 us
    psum x1 -> x2, waiting for transfers between devices: 161 us -> 140 us  [detail_sectors_over_axis(): panel = lax.psum(panel, at)]
    psum x1 -> x2, blocking collectives: 76.8 us -> 83.6 us  [detail_sectors_over_axis(): panel = lax.psum(panel, at)]
  transfers between devices with their start and end apart: 5 -> 6, of which waited for: 4 -> 4; matrix products, arithmetic and copies ran while one was open for 6% -> 7% of each run, Pallas kernels for 0% -> 0%
where the time goes in v1:
time: 699 us; the launch traced here: 692 us
  waiting for transfers between devices  211 us (30%)
  matrix products  158 us (23%)
  other arithmetic  141 us (20%)
  blocking collectives  83.6 us (12%)
  local copies, waits for them, and re-layouts  54 us (8%)
  starting transfers between devices  27 us (4%)
  between operations  14.5 us (2%)
    psum x2, waiting for transfers between devices, detail_sectors_over_axis(): panel = lax.psum(panel, at)  140 us
    psum x2, blocking collectives, detail_sectors_over_axis(): panel = lax.psum(panel, at)  83.6 us
    all_to_all x4, waiting for transfers between devices, swap_slots(): lax.all_to_all(blocks, ('outer', 'link'), split_axis=0, concat_axis=0, ti...  71.7 us
    dot_general x48, matrix products, gate_terms(): jnp.dot(hop_input, input_weight, preferred_element_type=jnp.float32)  31.8 us
    dot_general x48, matrix products, gate_terms(): jnp.dot(state_now.astype(jnp.bfloat16), hidden_weight, preferred_element_...  31.7 us
    dot_general x24, matrix products, back_step(): jnp.dot(state_now.astype(jnp.bfloat16).T, hid_bf, preferred_element_type=...  31 us
    dot_general x24, matrix products, back_step(): jnp.dot(hop_input.T, in_bf, preferred_element_type=jnp.float32)  29.4 us
    all_to_all x4, starting transfers between devices, swap_slots(): lax.all_to_all(blocks, ('outer', 'link'), split_axis=0, concat_axis=0, ti...  26.7 us
  transfers between devices with their start and end apart: 6, of which 4 were waited for; matrix products, arithmetic and copies ran while one was open for 7% of the time, Pallas kernels for 0%

profile of v1, /device:TPU:2, one launch (start us, length us, event | category | flops | bytes accessed | tf_op | source)
XLA Modules:
  0.0 692.0 jit_solution(12242869880465089097)
XLA Ops:
  8.8 7.6 %gather_fusion = bf16[2048,256]{1,0:T(8,128)(2,1)S(1)} fusion(bf16[512,256]{1,0:T(8,128)(2,1)} %bitcast.135, s32[2048]{0:T(1024)S(1)} %broadcast_clamp_fusion), kind=kCustom, calls=%fused_computation.clone | custom fusion | bytes 2105344 | tf_op jit(solution)/shard_map/jit(_take)/gather | solution.py:193
  16.4 1.2 broadcast_select_fusion.2
  17.7 11.5 %all-to-all-start = ((bf16[32,64,256]{2,1,0:T(8,128)(2,1)}), bf16[32,64,256]{2,1,0:T(8,128)(2,1)S(1)}, u32[]{:S(2)}, u32[]{:S(2)}) async-start(bf16[32,64,256]{2,1,0:T(8,128)(2,1)} %broadcast_select_fusion.2), calls=%async_computation | async-start | bytes 2097152 | tf_op jit(solution)/shard_map/all_to_all | solution.py:155
  29.9 27.9 %all-to-all-done = bf16[32,64,256]{2,1,0:T(8,128)(2,1)S(1)} async-done(((bf16[32,64,256]{2,1,0:T(8,128)(2,1)}), bf16[32,64,256]{2,1,0:T(8,128)(2,1)S(1)}, u32[]{:S(2)}, u32[]{:S(2)}) %all-to-all-start) | async-done | bytes 1048608 | tf_op jit(solution)/shard_map/all_to_all | solution.py:155
  57.8 13.0 %gather_fusion.1 = bf16[3072,256]{1,0:T(8,128)(2,1)} fusion(bf16[2048,256]{1,0:T(8,128)(2,1)S(1)} %bitcast.137, s32[3072]{0:T(1024)S(1)} %bitcast_clamp_fusion), kind=kCustom, calls=%fused_computation.1.clone | custom fusion | bytes 3158016 | tf_op jit(solution)/shard_map/jit(_take)/gather | solution.py:194
  70.7 1.7 broadcast_select_fusion
  72.5 2.0 broadcast.84.clone
  74.6 29.4 %while.35 = (s32[]{:T(128)}, f32[128,256]{1,0:T(8,128)S(1)}, f32[24,128,256]{2,1,0:T(8,128)}, f32[24,128]{1,0:T(8,128)S(1)}, bf16[24,128,256]{2,1,0:T(8,128)(2,1...) while((s32[]{:T(128)}, f32[128,256]{1,0:T(8,128)S(1)}, ...), condition=%wide.region_1.4_spmd, body=%wide.region_0.3_spmd.sunk | while | flops 101253248 | bytes 2954097 | solution.py:36
  104.0 4.6 broadcast_multiply_fusion
  108.5 17.9 %scatter_custom_fusion = f32[2048,256]{1,0:T(8,128)S(1)} fusion(s32[3072]{0:T(1024)S(1)} %bitcast.155, f32[3072,256]{1,0:T(8,128)} %bitcast.148, f32[]{:T(128)} %constant.108.clone.1), kind=kCustom, calls=%fused_computation.102 | custom fusion | flops 786432 | bytes 2097664 | tf_op jit(solution)/shard_map/scatter-add | solution.py:196
  127.6 5.2 all-to-all-start.1
  135.5 25.6 %all-to-all-done.1 = bf16[32,64,256]{2,1,0:T(8,128)(2,1)S(1)} async-done(((bf16[32,64,256]{2,1,0:T(8,128)(2,1)}), bf16[32,64,256]{2,1,0:T(8,128)(2,1)S(1)}, u32[]{:S(2)}, u32[]{:S(2)}) %all-to-all-start.1) | async-done | bytes 1048608 | tf_op jit(solution)/shard_map/all_to_all | solution.py:155
  161.1 11.9 %scatter_custom_fusion.1 = f32[512,256]{1,0:T(8,128)S(1)} fusion(s32[2048]{0:T(1024)} %reshape.174, bf16[2048,256]{1,0:T(8,128)(2,1)S(1)} %bitcast.146, f32[]{:T(128)} %constant.108.clone.1), kind=kCustom, calls=%fused_computation.84 | custom fusion | flops 1048576 | bytes 1573376 | tf_op jit(solution)/shard_map/scatter-add | solution.py:202
  173.9 2.1 fusion.85
  177.0 7.5 %gather_fusion.2 = bf16[2048,256]{1,0:T(8,128)(2,1)S(1)} fusion(bf16[512,256]{1,0:T(8,128)(2,1)S(1)} %convolution_convert_fusion, s32[2048]{0:T(1024)S(1)} %broadcast_clamp_fusion), kind=kCustom, calls=%fused_computation.2.clone | custom fusion | bytes 2105344 | tf_op jit(solution)/shard_map/jit(_take)/gather | solution.py:216
  184.5 1.2 broadcast_select_fusion.1
  185.7 4.9 all-to-all-start.2
  192.7 1.5 bitcast_convert_fusion.3
  194.2 2.1 slice.91
  196.3 1.8 pad_maximum_fusion.1
  200.7 18.2 %all-to-all-done.2 = bf16[32,64,256]{2,1,0:T(8,128)(2,1)S(1)} async-done(((bf16[32,64,256]{2,1,0:T(8,128)(2,1)}), bf16[32,64,256]{2,1,0:T(8,128)(2,1)S(1)}, u32[]{:S(2)}, u32[]{:S(2)}) %all-to-all-start.2) | async-done | bytes 1048608 | tf_op jit(solution)/shard_map/all_to_all | solution.py:155
  218.9 12.9 %gather_fusion.3 = bf16[3072,256]{1,0:T(8,128)(2,1)} fusion(bf16[2048,256]{1,0:T(8,128)(2,1)S(1)} %bitcast.136, s32[3072]{0:T(1024)S(1)} %copy-done.32), kind=kCustom, calls=%fused_computation.3.clone | custom fusion | bytes 3158016 | tf_op jit(solution)/shard_map/jit(_take)/gather | solution.py:218
  231.9 4.1 convert_multiply_fusion
  236.0 2.1 broadcast.84
  238.1 176.1 %while.36 = (s32[]{:T(128)}, f32[128,256]{1,0:T(8,128)S(1)}, f32[256,768]{1,0:T(8,128)S(1)}, f32[256,768]{1,0:T(8,128)S(1)}, f32[768]{0:T(1024)S(1)}, /*index=5*...) while((s32[]{:T(128)}, f32[128,256]{1,0:T(8,128)S(1)}, ...), condition=%wide.region_6.9_spmd.clone, body=%wide.region_4.8_spmd.clone.sunk | while | flops 306152320 | bytes 12996093 | solution.py:108
  242.0 1.3 convolution_add_fusion.15
  243.3 1.2 convolution_add_fusion.14
  249.3 1.3 convolution_add_fusion.15
  256.7 1.3 convolution_add_fusion.15
  264.0 1.3 convolution_add_fusion.15
  265.3 1.2 convolution_add_fusion.14
  271.3 1.3 convolution_add_fusion.15
  272.6 1.2 convolution_add_fusion.14
  278.6 1.3 convolution_add_fusion.15
  279.9 1.2 convolution_add_fusion.14
  286.0 1.3 convolution_add_fusion.15
  293.3 1.3 convolution_add_fusion.15
  300.7 1.3 convolution_add_fusion.15
  308.0 1.3 convolution_add_fusion.15
  315.3 1.3 convolution_add_fusion.15
  322.7 1.3 convolution_add_fusion.15
  330.0 1.3 convolution_add_fusion.15
  337.4 1.3 convolution_add_fusion.15
  344.7 1.3 convolution_add_fusion.15
  352.0 1.3 convolution_add_fusion.15
  359.4 1.3 convolution_add_fusion.15
  366.7 1.3 convolution_add_fusion.15
  368.0 1.2 convolution_add_fusion.14
  374.0 1.3 convolution_add_fusion.15
  381.4 1.3 convolution_add_fusion.15
  382.7 1.2 convolution_add_fusion.14
  388.7 1.3 convolution_add_fusion.15
  396.0 1.3 convolution_add_fusion.15
  403.4 1.3 convolution_add_fusion.15
  410.7 1.3 convolution_add_fusion.15
  415.3 17.9 %scatter_custom_fusion.2 = f32[2048,256]{1,0:T(8,128)S(1)} fusion(s32[3072]{0:T(1024)} %bitcast.154, f32[3072,256]{1,0:T(8,128)} %bitcast.147, f32[]{:T(128)} %constant.108.clone.1), kind=kCustom, calls=%fused_computation.100 | custom fusion | flops 786432 | bytes 2097664 | tf_op jit(solution)/shard_map/scatter-add | solution.py:226
  434.3 5.1 all-to-all-start.3
  439.5 139.5 %all-reduce.7.cloned.1.call-done = (f32[256,768]{1,0:T(8,128)}, f32[256,768]{1,0:T(8,128)}, f32[512,256]{1,0:T(8,128)}, f32[256,256]{1,0:T(8,128)}) async-done(((f32[256,768]{1,0:T(8,128)}, f32[256,768]{1,0:T(8,128)}, f32[512,256]{1,0:T(8,128)}, f32[256,256]{1,0:T(8,128)}), (f32[256,768]{1,0:T(8,128)}, f32[256,768]{1,0:T(8,128)}, f32[512,256]{1,0:T(8,128)}, ...) | async-done | bytes 2359312 | tf_op jit(solution)/shard_map/psum | solution.py:178
  579.1 1.5 slice.215
  582.0 73.4 %all-reduce = (f32[768]{0:T(1024)S(1)}, f32[256]{0:T(256)S(1)}, f32[256]{0:T(256)S(1)}) all-reduce(f32[768]{0:T(1024)S(1)} %get-tuple-element.357, f32[256]{0:T(256)S(1)} %copy-done.39, f32[256]{0:T(256)S(1)} %fusion.64), channel_id=1, replica_groups=mesh['replica'=8,'outer'=4,'link'=8] {'outer','link'}, use_global_device_ids=true, to_apply=%region_13.16 | all-reduce | flops 1280 | bytes 10240 | tf_op jit(solution)/shard_map/psum | solution.py:178
  655.4 10.2 %all-reduce.2 = (f32[768]{0:T(1024)S(1)}, f32[256]{0:T(256)S(1)}, f32[256]{0:T(256)S(1)}) all-reduce(f32[768]{0:T(1024)S(1)} %get-tuple-element.452, f32[256]{0:T(256)S(1)} %get-tuple-element.453, f32[256]{0:T(256)S(1)} %get-tuple-element.454), channel_id=1, replica_groups=mesh['replica'=8,'outer'=4,'link'=8] {'replica'}, use_global_device_ids=true, to_apply=%region_14.17 | all-reduce | flops 1280 | bytes 10240 | tf_op jit(solution)/shard_map/psum | solution.py:178
  667.4 12.0 %scatter_custom_fusion.3 = f32[512,256]{1,0:T(8,128)S(1)} fusion(f32[512,256]{1,0:T(8,128)S(1)} %convolution_add_fusion.5, s32[2048]{0:T(1024)} %reshape.174, bf16[2048,256]{1,0:T(8,128)(2,1)S(1)} %bitcast.145), kind=kCustom, calls=%fused_computation.82 | custom fusion | flops 1048576 | bytes 1572864 | tf_op jit(solution)/shard_map/scatter-add | solution.py:232
  679.4 2.3 broadcast_multiply_fusion.2
  681.7 1.7 broadcast_multiply_fusion.4
  (523 shorter events, 184.5 us)
Async XLA Ops:
  7.2 166.7 %copy-start = (bf16[256,256]{1,0:T(8,128)(2,1)S(1)}, bf16[256,256]{1,0:T(8,128)(2,1)}, u32[]{:S(2)}) copy-start(bf16[256,256]{1,0:T(8,128)(2,1)} %param.36) | copy-start | bytes 393220
  16.4 12.8 %copy-start.34 = (s32[1,128,24]{1,2,0:T(8,128)S(1)}, s32[1,128,24]{1,2,0:T(8,128)}, u32[]{:S(2)}) copy-start(s32[1,128,24]{1,2,0:T(8,128)} %param.25) | copy-start | bytes 36868
  16.4 12.8 %copy-start.40 = (s32[1,128]{1,0:T(1,128)S(1)}, s32[1,128]{1,0:T(1,128)}, u32[]{:S(2)}) copy-start(s32[1,128]{1,0:T(1,128)} %param.26) | copy-start | bytes 1540
  16.4 12.8 %copy-start.33 = (bf16[1,128,256]{2,1,0:T(8,128)(2,1)S(1)}, bf16[1,128,256]{2,1,0:T(8,128)(2,1)}, u32[]{:S(2)}) copy-start(bf16[1,128,256]{2,1,0:T(8,128)(2,1)} %param.24) | copy-start | bytes 196612
  17.7 40.1 %all-to-all-start = ((bf16[32,64,256]{2,1,0:T(8,128)(2,1)}), bf16[32,64,256]{2,1,0:T(8,128)(2,1)S(1)}, u32[]{:S(2)}, u32[]{:S(2)}) async-start(bf16[32,64,256]{2,1,0:T(8,128)(2,1)} %broadcast_select_fusion.2), calls=%async_computation | async-start | bytes 2097152 | tf_op jit(solution)/shard_map/all_to_all | solution.py:155
  29.2 41.6 %copy-start.31 = (s32[3072]{0:T(1024)}, s32[3072]{0:T(1024)S(1)}, u32[]{:S(2)}) copy-start(s32[3072]{0:T(1024)S(1)} %bitcast_clamp_fusion) | copy-start | bytes 36868
  29.2 41.5 %copy-start.35 = (pred[24,128]{1,0:T(8,128)(4,1)}, pred[24,128]{1,0:T(8,128)(4,1)S(1)}, u32[]{:S(2)}) copy-start(pred[24,128]{1,0:T(8,128)(4,1)S(1)} %get-tuple-element.481) | copy-start | bytes 9220
  72.5 2.1 copy-start.2
  72.5 2.1 copy-start.3
  72.5 2.1 copy-start.25
  104.0 4.6 copy-start.12
  104.0 4.6 copy-start.29
  126.5 8.8 %copy-start.1 = (bf16[1,512,256]{2,1,0:T(8,128)(2,1)S(1)}, bf16[1,512,256]{2,1,0:T(8,128)(2,1)}, u32[]{:S(2)}) copy-start(bf16[1,512,256]{2,1,0:T(8,128)(2,1)} %param.23) | copy-start | bytes 786436
  126.5 8.8 %copy-start.13 = (bf16[512,256]{1,0:T(8,128)(2,1)S(1)}, bf16[512,256]{1,0:T(8,128)(2,1)}, u32[]{:S(2)}) copy-start(bf16[512,256]{1,0:T(8,128)(2,1)} %param.34) | copy-start | bytes 786436
  127.6 5.8 copy-start.28
  127.6 7.1 %copy-start.38 = (s32[1,512]{1,0:T(1,128)S(1)}, s32[1,512]{1,0:T(1,128)}, u32[]{:S(2)}) copy-start(s32[1,512]{1,0:T(1,128)} %param.27) | copy-start | bytes 6148
  127.6 45.4 %copy-start.14 = (bf16[512,256]{1,0:T(8,128)(2,1)S(1)}, bf16[512,256]{1,0:T(8,128)(2,1)}, u32[]{:S(2)}) copy-start(bf16[512,256]{1,0:T(8,128)(2,1)} %param.34) | copy-start | bytes 786436
  127.6 33.5 %all-to-all-start.1 = ((bf16[32,64,256]{2,1,0:T(8,128)(2,1)}), bf16[32,64,256]{2,1,0:T(8,128)(2,1)S(1)}, u32[]{:S(2)}, u32[]{:S(2)}) async-start(bf16[32,64,256]{2,1,0:T(8,128)(2,1)} %bitcast.142), calls=%async_computation.1 | async-start | bytes 2097152 | tf_op jit(solution)/shard_map/all_to_all | solution.py:155
  173.9 2.1 copy-start.19
  185.7 33.2 %all-to-all-start.2 = ((bf16[32,64,256]{2,1,0:T(8,128)(2,1)}), bf16[32,64,256]{2,1,0:T(8,128)(2,1)S(1)}, u32[]{:S(2)}, u32[]{:S(2)}) async-start(bf16[32,64,256]{2,1,0:T(8,128)(2,1)} %broadcast_select_fusion.1), calls=%async_computation.2 | async-start | bytes 2097152 | tf_op jit(solution)/shard_map/all_to_all | solution.py:155
  190.6 388.3 %all-reduce.7.cloned.1.call-start = ((), (), s32[]{:S(2)}) async-start(), calls=%async_computation.4 | async-start | bytes 4718592 | tf_op jit(solution)/shard_map/psum | solution.py:178
  194.2 2.1 copy-start.22
  196.3 1.8 copy-start.10
  198.7 20.2 %copy-start.32 = (s32[3072]{0:T(1024)S(1)}, s32[3072]{0:T(1024)}, u32[]{:S(2)}) copy-start(s32[3072]{0:T(1024)} %copy-done.31) | copy-start | bytes 36868
  218.9 12.9 %copy-start.30 = (f32[24,128]{1,0:T(8,128)S(1)}, f32[24,128]{1,0:T(8,128)}, u32[]{:S(2)}) copy-start(f32[24,128]{1,0:T(8,128)} %copy-done.29) | copy-start | bytes 36868
  218.9 13.0 %copy-start.36 = (pred[24,128]{1,0:T(8,128)(4,1)S(1)}, pred[24,128]{1,0:T(8,128)(4,1)}, u32[]{:S(2)}) copy-start(pred[24,128]{1,0:T(8,128)(4,1)} %copy-done.35) | copy-start | bytes 9220
  236.0 2.1 copy-start.5
  236.0 2.1 copy-start.7
  236.0 2.1 copy-start.26
  239.2 2.4 copy-start.27
  246.6 2.4 copy-start.27
  253.9 2.4 copy-start.27
  261.2 2.4 copy-start.27
  268.6 2.4 copy-start.27
  275.9 2.4 copy-start.27
  283.2 2.4 copy-start.27
  290.6 2.4 copy-start.27
  297.9 2.4 copy-start.27
  305.2 2.4 copy-start.27
  312.6 2.4 copy-start.27
  319.9 2.4 copy-start.27
  327.2 2.4 copy-start.27
  334.6 2.4 copy-start.27
  341.9 2.4 copy-start.27
  349.3 2.4 copy-start.27
  356.6 2.4 copy-start.27
  363.9 2.4 copy-start.27
  371.3 2.4 copy-start.27
  378.6 2.4 copy-start.27
  385.9 2.4 copy-start.27
  393.3 2.4 copy-start.27
  400.6 2.4 copy-start.27
  407.9 2.4 copy-start.27
  414.1 19.1 %copy-start.8 = (f32[128,256]{1,0:T(8,128)}, f32[128,256]{1,0:T(8,128)S(1)}, u32[]{:S(2)}) copy-start(f32[128,256]{1,0:T(8,128)S(1)} %get-tuple-element.354) | copy-start | bytes 393220
  434.3 144.6 %copy-start.17 = (bf16[1,512,256]{2,1,0:T(8,128)(2,1)S(1)}, bf16[1,512,256]{2,1,0:T(8,128)(2,1)}, u32[]{:S(2)}) copy-start(bf16[1,512,256]{2,1,0:T(8,128)(2,1)} %param.29) | copy-start | bytes 786436
  434.3 146.4 %copy-start.21 = (f32[512,256]{1,0:T(8,128)S(1)}, f32[512,256]{1,0:T(8,128)}, u32[]{:S(2)}) copy-start(f32[512,256]{1,0:T(8,128)} %copy-done.19) | copy-start | bytes 1572868
  434.3 146.4 %copy-start.41 = (f32[256]{0:T(256)S(1)}, f32[256]{0:T(256)}, u32[]{:S(2)}) copy-start(f32[256]{0:T(256)} %param.37) | copy-start | bytes 3076
  434.3 233.0 %all-to-all-start.3 = ((bf16[32,64,256]{2,1,0:T(8,128)(2,1)}), bf16[32,64,256]{2,1,0:T(8,128)(2,1)S(1)}, u32[]{:S(2)}, u32[]{:S(2)}) async-start(bf16[32,64,256]{2,1,0:T(8,128)(2,1)} %bitcast.141), calls=%async_computation.3 | async-start | bytes 2097152 | tf_op jit(solution)/shard_map/all_to_all | solution.py:155
  439.4 240.0 %all-reduce.9.cloned.1.call-start = ((), (), s32[]{:S(2)}) async-start(), calls=%async_computation.5 | async-start | bytes 4718592 | tf_op jit(solution)/shard_map/psum | solution.py:178
  579.0 2.7 copy-start.11
  579.0 2.7 copy-start.15
  679.3 5.8 copy-start.24
  679.4 4.0 copy-start.23
  679.4 4.8 copy-start.18
  (7 other events, 8.2 us)
Sparse Core Ops, SparseCore 0:
  415.4 163.4 all-reduce.6
  581.5 66.7 all-reduce.8
